TPU v7x, 32 devices: a whole 2x2x4 slice. The times are simulated.
32 devices in a mesh: rows: 8 (over y, x, core), rhs: 4 (over z).
Axes of the slice: x: 2, y: 2, z: 4, core: 2. Of those that a mesh axis runs over, the one named last changes fastest.
Arguments:
- samples: float32 [65536, 16], P(('rows', 'rhs')), may hold values from -5 to 5
- freq_table: float32 [4096, 16], replicated, may hold values from -3 to 3
- feature_seeds: int32 [512], replicated, may hold values from 0 to 4095
- phases: float32 [512], replicated, may hold values from -3.140625 to 3.140625
- treatment_features: bfloat16 [65536, 512], P('rows', 'rhs'), may hold values from -2.5 to 2.5, as said below
Outputs:
- coefficients: float32 [512, 512], replicated
- fitted: float32 [65536, 512], P(('rows', 'rhs'))
Inputs may be any that keep to these rules, and one draw needn't show every extreme that they name: `treatment_features`: treatment features depend on the instrument values.
All inputs are finite; a program needn't handle non-finite values.
Results may differ from a plain program's by a relative error of at most 0.0008.
The roundings to bfloat16 on the way count: a program that leaves them out, or rounds other values in their place, can miss the bound.
Values may be sent and summed in bfloat16 or wider, within the bound.
A program may use at most 64 MiB of HBM per device.

v0:
```python
import jax
import jax.numpy as jnp
from jax import lax
from jax.sharding import PartitionSpec as P

ridge = 0.05


def solve_with(factor, right):
    lower = lax.linalg.triangular_solve(factor, right, left_side=True, lower=True)
    return lax.linalg.triangular_solve(factor, lower, left_side=True, lower=True, transpose_a=True)


def features_of(values, freqs, phases):
    angles = (
        jnp.dot(
            values, freqs.T, precision=lax.Precision.HIGHEST, preferred_element_type=jnp.float32
        )
        + phases
    )
    return (jnp.sqrt(jnp.float32(2.0)) * jnp.cos(angles)).astype(jnp.bfloat16)


def body(samples, freq_table, feature_seeds, phases, treatment_features):
    own_rows = samples.shape[0]
    count = own_rows * lax.axis_size("rows") * lax.axis_size("rhs")
    freqs = freq_table[feature_seeds]
    contract = (((0,), (0,)), ((), ()))
    instruments = features_of(samples, freqs, phases)
    gram_part = lax.dot_general(
        instruments, instruments, contract, preferred_element_type=jnp.float32
    )
    gram = lax.psum(gram_part, ("rows", "rhs")) / count
    gram = gram + ridge * jnp.eye(gram.shape[0], dtype=jnp.float32)
    factor = jnp.linalg.cholesky(gram)
    targets = lax.all_to_all(treatment_features, "rhs", split_axis=0, concat_axis=1, tiled=True)
    cross_part = lax.dot_general(instruments, targets, contract, preferred_element_type=jnp.float32)
    cross = lax.psum(cross_part, ("rows", "rhs")) / count
    coefficients = solve_with(factor, cross)
    fitted = jnp.dot(
        instruments, coefficients.astype(jnp.bfloat16), preferred_element_type=jnp.float32
    )
    return (coefficients, fitted)


def solution(mesh):
    placed = (P(("rows", "rhs"), None), P(), P(), P(), P("rows", "rhs"))
    return jax.shard_map(
        body, mesh=mesh, in_specs=placed, out_specs=(P(), P(("rows", "rhs"), None)), check_vma=False
    )
```

profile of v0, /device:TPU:0, one launch (start us, length us, event | category | flops | bytes accessed | tf_op | source)
XLA Modules:
  0.0 364.8 jit_solution(18324534306063840201)
XLA Ops:
  7.2 6.5 %all-to-all-start = ((bf16[4,2048,128]{2,1,0:T(8,128)(2,1)}), bf16[4,2048,128]{2,1,0:T(8,128)(2,1)S(1)}, u32[]{:S(2)}, u32[]{:S(2)}) async-start(bf16[4,2048,128]{2,1,0:T(8,128)(2,1)} %bitcast.66), calls=%async_computation | async-start | bytes 4194304 | tf_op jit(solution)/shard_map/all_to_all | solution.py:36
  13.7 1.9 copy.31
  15.7 2.6 gather_fusion
  18.3 17.9 %multiply_convert_fusion = bf16[512,2048]{1,0:T(8,128)(2,1)S(1)} fusion(f32[512,16]{1,0:T(8,128)S(1)} %gather_fusion, f32[2048,16]{0,1:T(8,128)S(1)} %copy-done, f32[512]{0:T(512)S(1)} %copy-done.8), kind=kOutput, calls=%fused_computation.3 | convolution fusion | flops 204472320 | bytes 2263040 | tf_op jit(solution)/shard_map/dot_general | solution.py:16
  37.6 2.3 fusion.50
  39.8 22.0 %all-to-all-done = bf16[4,2048,128]{2,1,0:T(8,128)(2,1)S(1)} async-done(((bf16[4,2048,128]{2,1,0:T(8,128)(2,1)}), bf16[4,2048,128]{2,1,0:T(8,128)(2,1)S(1)}, u32[]{:S(2)}, u32[]{:S(2)}) %all-to-all-start) | async-done | bytes 2097184 | tf_op jit(solution)/shard_map/all_to_all | solution.py:36
  61.9 3.1 copy.42
  65.0 4.5 %fusion.51 = f32[512,512]{0,1:T(8,128)} fusion(bf16[512,2048]{1,0:T(8,128)(2,1)} %copy-done.3, bf16[2048,512]{0,1:T(8,128)(2,1)} %bitcast.67), kind=kOutput, calls=%fused_computation.97 | convolution fusion | flops 1073741824 | bytes 5242880 | tf_op jit(solution)/shard_map/dot_general | solution.py:37
  69.5 133.9 %all-reduce.4.cloned.1.call-done = (f32[512,512]{0,1:T(8,128)}, f32[512,512]{0,1:T(8,128)}) async-done(((f32[512,512]{0,1:T(8,128)}, f32[512,512]{0,1:T(8,128)}), (f32[512,512]{0,1:T(8,128)}, f32[512,512]{0,1:T(8,128)})) %all-reduce.4.cloned.1.call-update) | async-done | bytes 2097168 | tf_op jit(solution)/shard_map/psum | solution.py:38
  203.4 2.8 select_add_fusion
  206.2 1.6 copy.33
  209.1 11.7 %cholesky.103 = f32[128,128]{1,0:T(8,128)S(1)} custom-call(f32[128,128]{1,0:T(8,128)S(1)} %cholesky.263), custom_call_target="Cholesky" | custom-call | tf_op jit(solution)/shard_map/jit(cholesky)/cholesky | solution.py:35
  220.9 9.8 %custom-call.32 = f32[1,128,128]{1,2,0:T(8,128)S(1)} custom-call(f32[1,128,128]{2,1,0:T(8,128)S(1)} %get-tuple-element.39), custom_call_target="InvertDiagBlocksLowerTriangular" | custom-call | tf_op jit(solution)/shard_map/jit(cholesky)/cholesky | solution.py:35
  233.4 11.9 %cholesky.215 = f32[128,128]{1,0:T(8,128)S(1)} custom-call(f32[128,128]{1,0:T(8,128)S(1)} %cholesky.267), custom_call_target="Cholesky" | custom-call | tf_op jit(solution)/shard_map/jit(cholesky)/cholesky | solution.py:35
  245.4 9.8 %custom-call.33 = f32[1,128,128]{1,2,0:T(8,128)S(1)} custom-call(f32[1,128,128]{2,1,0:T(8,128)S(1)} %get-tuple-element.37), custom_call_target="InvertDiagBlocksLowerTriangular" | custom-call | tf_op jit(solution)/shard_map/jit(cholesky)/cholesky | solution.py:35
  255.7 1.5 convolution_subtract_fusion.7
  257.2 11.7 %cholesky.236 = f32[128,128]{1,0:T(8,128)S(1)} custom-call(f32[128,128]{1,0:T(8,128)S(1)} %cholesky.272), custom_call_target="Cholesky" | custom-call | tf_op jit(solution)/shard_map/jit(cholesky)/cholesky | solution.py:35
  269.1 9.8 %custom-call.34 = f32[1,128,128]{1,2,0:T(8,128)S(1)} custom-call(f32[1,128,128]{2,1,0:T(8,128)S(1)} %get-tuple-element.35), custom_call_target="InvertDiagBlocksLowerTriangular" | custom-call | tf_op jit(solution)/shard_map/jit(cholesky)/cholesky | solution.py:35
  280.5 11.9 %cholesky.253 = f32[128,128]{1,0:T(8,128)S(1)} custom-call(f32[128,128]{1,0:T(8,128)S(1)} %convolution_subtract_fusion.8), custom_call_target="Cholesky" | custom-call | tf_op jit(solution)/shard_map/jit(cholesky)/cholesky | solution.py:35
  297.9 8.9 %while.1 = (s32[]{:T(128)}, f32[512,512]{0,1:T(8,128)S(1)}, s32[4,2]{0,1:T(2,128)S(1)}, f32[4,128,128]{2,1,0:T(8,128)S(1)}, s32[]{:T(128)}) while((s32[]{:T(128)}, f32[512,512]{0,1:T(8,128)S(1)}, s32[4,2]{0,1:T(2,128)S(1)}, f32[4,128,128]{2,1,0:T(8,128)S(1)}, s32[]{:T(128)}) %tuple.30), condition=%wide.while_cond, body=%wide.while_body.sunk | while | flops 2 | bytes 393329 | solution.py:11
  298.6 1.4 dynamic-slice.7
  306.8 39.3 %custom-call.35 = f32[4,128,128]{1,2,0:T(8,128)S(1)} custom-call(f32[4,128,128]{2,1,0:T(8,128)S(1)} %get-tuple-element.9), custom_call_target="InvertDiagBlocksLowerTriangular" | custom-call | tf_op jit(solution)/shard_map/triangular_solve | solution.py:11
  349.0 1.5 convolution_subtract_fusion.5
  354.4 3.3 fusion.17
  (86 shorter events, 24.7 us)
Async XLA Ops:
  7.2 11.2 %copy-start = (f32[2048,16]{0,1:T(8,128)S(1)}, f32[2048,16]{0,1:T(8,128)}, u32[]{:S(2)}) copy-start(f32[2048,16]{0,1:T(8,128)} %param.5) | copy-start | bytes 393220
  7.2 6.6 %copy-start.6 = (f32[4096,16]{0,1:T(8,128)S(1)}, f32[4096,16]{0,1:T(8,128)}, u32[]{:S(2)}) copy-start(f32[4096,16]{0,1:T(8,128)} %param.6) | copy-start | bytes 786436
  7.2 54.7 %all-to-all-start = ((bf16[4,2048,128]{2,1,0:T(8,128)(2,1)}), bf16[4,2048,128]{2,1,0:T(8,128)(2,1)S(1)}, u32[]{:S(2)}, u32[]{:S(2)}) async-start(bf16[4,2048,128]{2,1,0:T(8,128)(2,1)} %bitcast.66), calls=%async_computation | async-start | bytes 4194304 | tf_op jit(solution)/shard_map/all_to_all | solution.py:36
  13.7 2.0 copy-start.7
  13.7 4.6 %copy-start.8 = (f32[512]{0:T(512)S(1)}, f32[512]{0:T(512)}, u32[]{:S(2)}) copy-start(f32[512]{0:T(512)} %param.8) | copy-start | bytes 6148
  13.7 189.7 %all-reduce.4.cloned.1.call-start = ((), (), s32[]{:S(2)}) async-start(), calls=%async_computation.1 | async-start | bytes 4194304 | tf_op jit(solution)/shard_map/psum | solution.py:38
  36.2 1.3 copy-start.3
  206.2 1.7 copy-start.2
  208.1 1.0 copy-start.5
  352.8 1.6 copy-start.4
  354.4 3.3 copy-start.1
Sparse Core Ops, SparseCore 0:
  69.6 133.7 all-reduce.3
where the time goes:
time: 369 us; the launch traced here: 365 us
  waiting for transfers between devices  156 us (42%)
  other arithmetic  122 us (33%)
  matrix products  41.5 us (11%)
  local copies, waits for them, and re-layouts  21.6 us (6%)
  between operations  17.2 us (5%)
  starting transfers between devices  6.53 us (2%)
    psum x1, waiting for transfers between devices, body(): cross = lax.psum(cross_part, ('rows', 'rhs')) / count  134 us
    another operation x15, other arithmetic, body(): factor = jnp.linalg.cholesky(gram)  79.4 us
    another operation x4, other arithmetic, solve_with(): lax.linalg.triangular_solve(factor, lower, left_side=True, lower=True, tr...  39.5 us
    all_to_all x1, waiting for transfers between devices, body(): lax.all_to_all(treatment_features, 'rhs', split_axis=0, concat_axis=1, ti...  22 us
    dot_general x1, matrix products, features_of(): jnp.dot(values, freqs.T, precision=lax.Precision.HIGHEST, preferred_eleme...  17.9 us
    another operation x20, local copies, waits for them, and re-layouts  8.79 us
  transfers between devices with their start and end apart: 2, of which 2 were waited for; matrix products, arithmetic and copies ran while one was open for 7% of the time, Pallas kernels for 0%

commit v1 on v0

--- a/solution.py
+++ b/solution.py
@@ -33,7 +33,12 @@
     gram = lax.psum(gram_part, ("rows", "rhs")) / count
     gram = gram + ridge * jnp.eye(gram.shape[0], dtype=jnp.float32)
     factor = jnp.linalg.cholesky(gram)
-    targets = lax.all_to_all(treatment_features, "rhs", split_axis=0, concat_axis=1, tiled=True)
+    targets = jnp.concatenate(
+        lax.all_to_all(
+            jnp.stack(jnp.split(treatment_features, lax.axis_size("rhs"), axis=0)), "rhs", 0, 0
+        ),
+        axis=1,
+    )
     cross_part = lax.dot_general(instruments, targets, contract, preferred_element_type=jnp.float32)
     cross = lax.psum(cross_part, ("rows", "rhs")) / count
     coefficients = solve_with(factor, cross)

time: 369 us -> 369 us (level)
  local copies, waits for them, and re-layouts: 21.6 us -> 16.2 us
  waiting for transfers between devices: 156 us -> 160 us
    all_to_all x1, waiting for transfers between devices: 22 us -> 25.9 us  [body(): lax.all_to_all(jnp.stack(jnp.split(treatment_features, lax.axis_size('rhs...]
  transfers between devices with their start and end apart: 2 -> 2, of which waited for: 2 -> 2; matrix products, arithmetic and copies ran while one was open for 7% -> 6% of each run, Pallas kernels for 0% -> 0%
where the time goes in v1:
time: 369 us; the launch traced here: 365 us
  waiting for transfers between devices  160 us (43%)
  other arithmetic  123 us (33%)
  matrix products  41.3 us (11%)
  between operations  17.2 us (5%)
  local copies, waits for them, and re-layouts  16.2 us (4%)
  starting transfers between devices  6.51 us (2%)
    psum x1, waiting for transfers between devices, body(): cross = lax.psum(cross_part, ('rows', 'rhs')) / count  134 us
    another operation x15, other arithmetic, body(): factor = jnp.linalg.cholesky(gram)  79.4 us
    another operation x4, other arithmetic, solve_with(): lax.linalg.triangular_solve(factor, lower, left_side=True, lower=True, tr...  39.5 us
    all_to_all x1, waiting for transfers between devices, body(): lax.all_to_all(jnp.stack(jnp.split(treatment_features, lax.axis_size('rhs...  25.9 us
    dot_general x1, matrix products, features_of(): jnp.dot(values, freqs.T, precision=lax.Precision.HIGHEST, preferred_eleme...  18.4 us
    another operation x20, local copies, waits for them, and re-layouts  8.21 us
  transfers between devices with their start and end apart: 2, of which 2 were waited for; matrix products, arithmetic and copies ran while one was open for 6% of the time, Pallas kernels for 0%

profile of v1, /device:TPU:0, one launch (start us, length us, event | category | flops | bytes accessed | tf_op | source)
XLA Modules:
  0.0 364.7 jit_solution(5109882198727694644)
XLA Ops:
  7.2 1.7 fusion.50
  9.8 1.6 pad_maximum_fusion
  11.4 6.5 %all-to-all-start = ((bf16[4,2048,128]{1,2,0:T(8,128)(2,1)}), bf16[4,2048,128]{1,2,0:T(8,128)(2,1)}, u32[]{:S(2)}, u32[]{:S(2)}) async-start(bf16[4,2048,128]{1,2,0:T(8,128)(2,1)} %pad_maximum_fusion), calls=%async_computation | async-start | bytes 4194304 | tf_op jit(solution)/shard_map/all_to_all | solution.py:37
  19.6 18.4 %multiply_convert_fusion = bf16[512,2048]{1,0:T(8,128)(2,1)S(1)} fusion(f32[512,16]{1,0:T(8,128)S(1)} %gather_fusion, f32[2048,16]{0,1:T(8,128)S(1)} %copy-done, f32[512]{0:T(512)S(1)} %copy-done.8), kind=kOutput, calls=%fused_computation.3 | convolution fusion | flops 204472320 | bytes 2263040 | tf_op jit(solution)/shard_map/dot_general | solution.py:16
  38.0 2.3 fusion.51
  40.3 25.9 %all-to-all-done = bf16[4,2048,128]{1,2,0:T(8,128)(2,1)} async-done(((bf16[4,2048,128]{1,2,0:T(8,128)(2,1)}), bf16[4,2048,128]{1,2,0:T(8,128)(2,1)}, u32[]{:S(2)}, u32[]{:S(2)}) %all-to-all-start) | async-done | bytes 2097184 | tf_op jit(solution)/shard_map/all_to_all | solution.py:37
  66.1 3.8 %fusion.52 = f32[512,512]{0,1:T(8,128)} fusion(bf16[512,2048]{1,0:T(8,128)(2,1)S(1)} %multiply_convert_fusion, bf16[2048,512]{0,1:T(8,128)(2,1)} %bitcast.13), kind=kOutput, calls=%fused_computation.99 | convolution fusion | flops 1073741824 | bytes 5242880 | tf_op jit(solution)/shard_map/dot_general | solution.py:42
  70.0 133.9 %all-reduce.4.cloned.1.call-done = (f32[512,512]{0,1:T(8,128)}, f32[512,512]{0,1:T(8,128)}) async-done(((f32[512,512]{0,1:T(8,128)}, f32[512,512]{0,1:T(8,128)}), (f32[512,512]{0,1:T(8,128)}, f32[512,512]{0,1:T(8,128)})) %all-reduce.4.cloned.1.call-update) | async-done | bytes 2097168 | tf_op jit(solution)/shard_map/psum | solution.py:43
  203.9 2.8 select_add_fusion
  206.7 1.6 copy.21
  209.5 11.7 %cholesky.103 = f32[128,128]{1,0:T(8,128)S(1)} custom-call(f32[128,128]{1,0:T(8,128)S(1)} %cholesky.263), custom_call_target="Cholesky" | custom-call | tf_op jit(solution)/shard_map/jit(cholesky)/cholesky | solution.py:35
  221.3 9.8 %custom-call.32 = f32[1,128,128]{1,2,0:T(8,128)S(1)} custom-call(f32[1,128,128]{2,1,0:T(8,128)S(1)} %get-tuple-element.39), custom_call_target="InvertDiagBlocksLowerTriangular" | custom-call | tf_op jit(solution)/shard_map/jit(cholesky)/cholesky | solution.py:35
  233.6 11.9 %cholesky.215 = f32[128,128]{1,0:T(8,128)S(1)} custom-call(f32[128,128]{1,0:T(8,128)S(1)} %cholesky.267), custom_call_target="Cholesky" | custom-call | tf_op jit(solution)/shard_map/jit(cholesky)/cholesky | solution.py:35
  245.9 9.8 %custom-call.33 = f32[1,128,128]{1,2,0:T(8,128)S(1)} custom-call(f32[1,128,128]{2,1,0:T(8,128)S(1)} %get-tuple-element.37), custom_call_target="InvertDiagBlocksLowerTriangular" | custom-call | tf_op jit(solution)/shard_map/jit(cholesky)/cholesky | solution.py:35
  256.2 1.5 convolution_subtract_fusion.7
  257.7 11.7 %cholesky.236 = f32[128,128]{1,0:T(8,128)S(1)} custom-call(f32[128,128]{1,0:T(8,128)S(1)} %cholesky.272), custom_call_target="Cholesky" | custom-call | tf_op jit(solution)/shard_map/jit(cholesky)/cholesky | solution.py:35
  269.6 9.8 %custom-call.34 = f32[1,128,128]{1,2,0:T(8,128)S(1)} custom-call(f32[1,128,128]{2,1,0:T(8,128)S(1)} %get-tuple-element.35), custom_call_target="InvertDiagBlocksLowerTriangular" | custom-call | tf_op jit(solution)/shard_map/jit(cholesky)/cholesky | solution.py:35
  281.0 11.9 %cholesky.253 = f32[128,128]{1,0:T(8,128)S(1)} custom-call(f32[128,128]{1,0:T(8,128)S(1)} %convolution_subtract_fusion.8), custom_call_target="Cholesky" | custom-call | tf_op jit(solution)/shard_map/jit(cholesky)/cholesky | solution.py:35
  298.3 8.4 %while.1 = (s32[]{:T(128)}, f32[512,512]{0,1:T(8,128)S(1)}, s32[4,2]{0,1:T(2,128)S(1)}, f32[4,128,128]{2,1,0:T(8,128)S(1)}, s32[]{:T(128)}) while((s32[]{:T(128)}, f32[512,512]{0,1:T(8,128)S(1)}, s32[4,2]{0,1:T(2,128)S(1)}, f32[4,128,128]{2,1,0:T(8,128)S(1)}, s32[]{:T(128)}) %tuple.32), condition=%wide.while_cond, body=%wide.while_body.sunk | while | flops 2 | bytes 393321 | solution.py:11
  301.0 1.4 dynamic-slice.7
  303.1 1.4 dynamic-slice.7
  306.7 39.3 %custom-call.35 = f32[4,128,128]{1,2,0:T(8,128)S(1)} custom-call(f32[4,128,128]{2,1,0:T(8,128)S(1)} %get-tuple-element.9), custom_call_target="InvertDiagBlocksLowerTriangular" | custom-call | tf_op jit(solution)/shard_map/triangular_solve | solution.py:11
  348.9 1.5 convolution_subtract_fusion.5
  354.3 3.3 fusion.17
  (91 shorter events, 24.0 us)
Async XLA Ops:
  7.2 12.4 %copy-start = (f32[2048,16]{0,1:T(8,128)S(1)}, f32[2048,16]{0,1:T(8,128)}, u32[]{:S(2)}) copy-start(f32[2048,16]{0,1:T(8,128)} %param.5) | copy-start | bytes 393220
  11.4 6.5 %copy-start.6 = (f32[4096,16]{0,1:T(8,128)S(1)}, f32[4096,16]{0,1:T(8,128)}, u32[]{:S(2)}) copy-start(f32[4096,16]{0,1:T(8,128)} %param.6) | copy-start | bytes 786436
  11.4 54.8 %all-to-all-start = ((bf16[4,2048,128]{1,2,0:T(8,128)(2,1)}), bf16[4,2048,128]{1,2,0:T(8,128)(2,1)}, u32[]{:S(2)}, u32[]{:S(2)}) async-start(bf16[4,2048,128]{1,2,0:T(8,128)(2,1)} %pad_maximum_fusion), calls=%async_computation | async-start | bytes 4194304 | tf_op jit(solution)/shard_map/all_to_all | solution.py:37
  17.8 0.7 copy-start.7
  17.8 1.8 copy-start.8
  17.8 186.1 %all-reduce.4.cloned.1.call-start = ((), (), s32[]{:S(2)}) async-start(), calls=%async_computation.1 | async-start | bytes 4194304 | tf_op jit(solution)/shard_map/psum | solution.py:43
  38.0 28.1 %copy-start.3 = (bf16[512,2048]{1,0:T(8,128)(2,1)}, bf16[512,2048]{1,0:T(8,128)(2,1)S(1)}, u32[]{:S(2)}) copy-start(bf16[512,2048]{1,0:T(8,128)(2,1)S(1)} %multiply_convert_fusion) | copy-start | bytes 6291460
  206.6 1.7 copy-start.2
  208.6 1.0 copy-start.5
  352.7 1.6 copy-start.4
  354.3 3.3 copy-start.1
Sparse Core Ops, SparseCore 0:
  70.1 133.7 all-reduce.3
